TPU v7x, 512 devices: a whole 4x4x16 slice. The times are simulated.
512 devices in a mesh: aux: 128 (over x, z, core), occ: 4 (over y).
Axes of the slice: x: 4, y: 4, z: 16, core: 2. Of those that a mesh axis runs over, the one named last changes fastest.
Arguments:
- half_ints: bfloat16 [8192, 3, 2560], P('aux', None, 'occ'), may hold values from -1.75 to 1.75
- coef_virt: bfloat16 [2048, 2560], P('aux', 'occ'), may hold values from -0.125 to 0.125
- screen: int32 [256, 20], P('aux', 'occ'), may hold values from 0 to 1, as said below
- occ_energy: float32 [512], replicated, may hold values from -2 to -0.3
- virt_energy: float32 [2048], replicated, may hold values from 0.2 to 4
- batch_orbitals: int32 [3], replicated, may hold values from 0 to 511, as said below
Outputs:
- amplitudes: float32 [128, 3, 256, 3, 128], P('aux', None, 'occ')
- gamma: bfloat16 [8192, 3, 2048], P(('aux', 'occ'))
Inputs may be any that keep to these rules, and one draw needn't show every extreme that they name: `screen`: 1 where a block of 32 auxiliary and 128 atomic functions is kept, 0 where it is screened out. `batch_orbitals`: 3 distinct occupied orbitals, among them the first and the last.
All inputs are finite; a program needn't handle non-finite values.
Results may differ from a plain program's by a relative error of at most 0.006.
Values may be sent and summed in bfloat16 or wider, within the bound.
No kernel may reach another device: no remote copies, remote signals or barrier semaphores. Data moves between devices by JAX's collectives and lax.ppermute only.
A program may use at most 64 MiB of HBM per device.

v0:
```python
import jax
import jax.numpy as jnp
from jax import lax
from jax.sharding import Mesh
from jax.sharding import PartitionSpec as P

BF = jnp.bfloat16
F32 = jnp.float32


def swap_cores(value):
    return lax.ppermute(value, "c", [(0, 1), (1, 0)])


def exchange(value, axis):
    members, rows, lanes = value.shape
    value = value.reshape(members * rows, lanes)
    value = lax.all_to_all(value, axis, split_axis=0, concat_axis=0, tiled=True)
    return value.reshape(members, rows, lanes)


def by_core(mine, theirs, core):
    return (jnp.where(core == 0, mine, theirs), jnp.where(core == 0, theirs, mine))


def local(half_ints, coef_virt, screen, occ_energy, virt_energy, batch_orbitals):
    p_rows, nocc, ao_part = half_ints.shape
    nv = virt_energy.shape[0]
    nx, nz, ny = (lax.axis_size("x"), lax.axis_size("z"), lax.axis_size("y"))
    nl = nz // 2
    x, z, c, y = (lax.axis_index(name) for name in ("x", "z", "c", "y"))
    zh, zl = (z // nl, z % nl)
    r = p_rows // ny
    wide = nv // nx
    narrow = nv // nz
    half = wide // 2
    share = half // ny
    ways = wide // narrow
    labels = jnp.arange(occ_energy.shape[0], dtype=jnp.int32)
    onehot = (batch_orbitals[:, None] == labels[None, :]).astype(F32)
    slot_energy = jnp.sum(onehot * occ_energy[None, :], axis=1)
    with jax.named_scope("transform"):
        copies = jnp.broadcast_to(coef_virt[None], (nz,) + coef_virt.shape)
        coef = exchange(copies, "z")
        expanded = jnp.repeat(jnp.repeat(screen, 32, axis=0), 128, axis=1).astype(BF)
        masked = half_ints * expanded[:, None, :]
        masked = masked.reshape(ny, r, nocc, ao_part).transpose(0, 2, 1, 3)
        masked = lax.all_gather(masked.reshape(-1, ao_part), "x", axis=0)
        masked = masked.reshape(nx, ny, nocc, r, ao_part)
        masked, coef = lax.optimization_barrier((masked, coef))
        low, high = by_core(coef, swap_cores(coef), c)
        coef = jnp.stack([low, high], axis=1).reshape(wide, ao_part)
        part = jnp.einsum("xyirm,am->yxira", masked, coef, preferred_element_type=F32)
        part = exchange(part.astype(BF).reshape(ny, nx * nocc * r, wide), "y")
        three = jnp.sum(part.astype(F32), axis=0).astype(BF).reshape(nx, nocc, r, wide)
    with jax.named_scope("panels"):
        row = jnp.concatenate([three[:, i] for i in range(nocc)], axis=-1)
        row = lax.all_gather(row.reshape(nx * r, nocc * wide), "z", axis=0, tiled=True)
        col = exchange(three.reshape(nx, nocc * r, wide), "x")
        col = col.reshape(nx, nocc, r, ways // 2, 2, narrow)
        col = jnp.concatenate(
            [col[:, i].transpose(3, 0, 2, 1, 4).reshape(nz, r, narrow) for i in range(nocc)],
            axis=-1,
        )
        col = exchange(col, "z")
        col = lax.all_gather(col.reshape(nz * r, nocc * narrow), "x", axis=0)
        col = col.reshape(nx, nz, r, nocc * narrow)
        col = col.transpose(1, 0, 2, 3).reshape(nz * nx * r, nocc * narrow)
    with jax.named_scope("gram"):
        gram = lax.dot_general(row, col, (((0,), (0,)), ((), ())), preferred_element_type=F32)
        gram = gram.reshape(nocc, 2, half, nocc * narrow)
        mine = lax.dynamic_index_in_dim(gram, c, 1, keepdims=False)
        other = lax.dynamic_index_in_dim(gram, 1 - c, 1, keepdims=False)
        gram = mine + swap_cores(other)
        gram = gram.reshape(nocc, ny, share, nocc * narrow).transpose(1, 0, 2, 3)
        gram = exchange(gram.astype(BF).reshape(ny, nocc * share, nocc * narrow), "y")
        gram = jnp.sum(gram.astype(F32), axis=0).reshape(nocc, share, nocc, narrow)
    with jax.named_scope("amplitudes"):
        row_energy = lax.dynamic_slice_in_dim(
            virt_energy, x * wide + c * half + y * share, share, 0
        )
        col_energy = lax.dynamic_slice_in_dim(virt_energy, (zl * 2 + zh) * narrow, narrow, 0)
        denominators = (
            slot_energy[:, None, None, None]
            + slot_energy[None, None, :, None]
            - row_energy[None, :, None, None]
            - col_energy[None, None, None, :]
        )
        amps = gram / denominators
        mixed = (2.0 * amps - jnp.transpose(amps, (2, 1, 0, 3))).astype(BF)
        swap = []
        for h in range(2):
            for l in range(nl):
                for k in range(2):
                    swap.append(((h * nl + l) * 2 + k, (k * nl + l) * 2 + h))
        own = lax.ppermute(amps, ("z", "c"), swap)
        mixed = jnp.concatenate([mixed[:, :, j] for j in range(nocc)], axis=-1)
        mixed = lax.all_gather(mixed.reshape(nocc * share, nocc * narrow), "y", axis=0)
        mixed = mixed.reshape(ny, nocc, share, nocc * narrow).transpose(1, 0, 2, 3)
        mixed = mixed.reshape(nocc, half, nocc * narrow)
        low, high = by_core(mixed, swap_cores(mixed), c)
        mixed = jnp.stack([low, high], axis=1).reshape(nocc * wide, nocc * narrow)
    with jax.named_scope("gamma"):
        value = jnp.dot(row, mixed, preferred_element_type=F32).astype(BF)
        value = value.reshape(nz, nx, r, nocc * narrow).transpose(1, 0, 2, 3)
        value = exchange(value.reshape(nx, nz * r, nocc * narrow), "x")
        value = jnp.sum(value.astype(F32), axis=0).astype(BF)
        value = exchange(value.reshape(nz, r, nocc * narrow), "z")
        value = value.reshape(2, nl, r, nocc, narrow).transpose(2, 3, 1, 0, 4)
        gamma = value.reshape(r, nocc, nv)
    return (own[None], gamma)


def solution(mesh):
    fine = Mesh(
        mesh.devices.reshape(4, mesh.shape["aux"] // 8, 2, mesh.shape["occ"]), ("x", "z", "c", "y")
    )
    aux = ("x", "z", "c")
    in_specs = (P(aux, None, "y"), P(aux, "y"), P(aux, "y"), P(), P(), P())
    out_specs = (P(aux, None, "y", None, None), P(aux + ("y",), None, None))
    return jax.shard_map(local, mesh=fine, in_specs=in_specs, out_specs=out_specs, check_vma=False)
```

profile of v0, /device:TPU:1, one launch (start us, length us, event | category | flops | bytes accessed | tf_op | source)
XLA Modules:
  0.0 264.1 jit_solution(2619876952096611985)
XLA Ops:
  7.2 1.5 broadcast_in_dim.10
  8.7 15.7 %all-to-all-start = ((bf16[16,16,640]{2,1,0:T(8,128)(2,1)}), bf16[16,16,640]{2,1,0:T(8,128)(2,1)S(1)}, u32[]{:S(2)}, u32[]{:S(2)}) async-start(bf16[16,16,640]{2,1,0:T(8,128)(2,1)} %broadcast_in_dim.10), calls=%async_computation | async-start | bytes 655360 | tf_op jit(solution)/shard_map/transform/all_to_all | solution.py:18
  24.4 0.0 all-gather.2.cloned.1.call-start
  24.5 0.7 convert_element_type.44
  25.2 0.1 broadcast_in_dim.9
  25.4 13.2 %all_gather.12 = bf16[4,192,640]{2,1,0:T(8,128)(2,1)S(1)} all-gather(bf16[1,192,640]{2,1,0:T(8,128)(2,1)S(1)} %bitcast.110), channel_id=1, replica_groups=mesh['x'=4,'z'=16,'c'=2,'y'=4] {'x'}, dimensions={0}, use_global_device_ids=true | all-gather | bytes 1228800 | tf_op jit(solution)/shard_map/transform/all_gather | solution.py:48
  38.7 1.0 all-to-all-done
  39.7 8.4 %collective-permute-start = (bf16[16,16,640]{2,1,0:T(8,128)(2,1)S(1)}, bf16[16,16,640]{2,1,0:T(8,128)(2,1)S(1)}, u32[]{:S(2)}, u32[]{:S(2)}) collective-permute-start(bf16[16,16,640]{2,1,0:T(8,128)(2,1)S(1)} %all-to-all-done), channel_id=1, source_target_pairs={{0,4},{4,0},{1,5},{5,1},{2,6},{6,2},{3,7},{7,3},{8,12},{12,8},{9,1... | collective-permute-start | bytes 983048 | tf_op jit(solution)/shard_map/transform/ppermute | solution.py:12
  48.1 1.2 collective-permute-done
  49.3 0.1 select_bitcast_fusion.3
  49.4 0.1 pad_maximum_fusion.1
  49.5 0.8 fusion
  50.3 0.1 copy.56
  50.3 15.4 %all_to_all.57 = bf16[4,192,512]{2,1,0:T(8,128)(2,1)S(1)} all-to-all(bf16[4,192,512]{2,1,0:T(8,128)(2,1)S(1)} %bitcast.100), channel_id=1, replica_groups=mesh['x'=4,'z'=16,'c'=2,'y'=4] {'y'}, dimensions={0} | all-to-all | bytes 1572864 | tf_op jit(solution)/shard_map/transform/all_to_all | solution.py:18
  65.7 0.1 reduce_sum.42
  65.9 0.7 pad_maximum_fusion.2
  66.6 9.0 %all_to_all.58 = bf16[4,48,512]{2,1,0:T(8,128)(2,1)S(1)} all-to-all(bf16[4,48,512]{2,1,0:T(8,128)(2,1)S(1)} %bitcast.107), channel_id=1, replica_groups=mesh['x'=4,'z'=16,'c'=2,'y'=4] {'x'}, dimensions={0} | all-to-all | bytes 393216 | tf_op jit(solution)/shard_map/panels/all_to_all | solution.py:18
  75.6 0.1 reshape.175
  75.7 0.2 slice_bitcast_fusion.2
  75.9 0.7 pad_maximum_fusion.3
  76.6 6.7 %all-to-all-start.3 = ((bf16[16,16,384]{2,1,0:T(8,128)(2,1)}), bf16[16,16,384]{2,1,0:T(8,128)(2,1)S(1)}, u32[]{:S(2)}, u32[]{:S(2)}) async-start(bf16[16,16,384]{2,1,0:T(8,128)(2,1)} %pad_maximum_fusion.3), calls=%async_computation.3 | async-start | bytes 393216 | tf_op jit(solution)/shard_map/panels/all_to_all | solution.py:18
  83.3 15.0 %all-to-all-done.3 = bf16[16,16,384]{2,1,0:T(8,128)(2,1)S(1)} async-done(((bf16[16,16,384]{2,1,0:T(8,128)(2,1)}), bf16[16,16,384]{2,1,0:T(8,128)(2,1)S(1)}, u32[]{:S(2)}, u32[]{:S(2)}) %all-to-all-start.3) | async-done | bytes 196640 | tf_op jit(solution)/shard_map/panels/all_to_all | solution.py:18
  98.3 11.9 %all_gather.14 = bf16[4,256,384]{2,1,0:T(8,128)(2,1)S(1)} all-gather(bf16[1,256,384]{2,1,0:T(8,128)(2,1)S(1)} %bitcast.115), channel_id=1, replica_groups=mesh['x'=4,'z'=16,'c'=2,'y'=4] {'x'}, dimensions={0}, use_global_device_ids=true | all-gather | bytes 983040 | tf_op jit(solution)/shard_map/panels/all_gather | solution.py:66
  110.1 1.0 copy.61
  111.2 25.6 %all-gather.2.cloned.1.call-done = bf16[1024,1536]{1,0:T(8,128)(2,1)} async-done(((bf16[64,1536]{1,0:T(8,128)(2,1)}), bf16[1024,1536]{1,0:T(8,128)(2,1)}) %all-gather.2.cloned.1.call-update) | async-done | bytes 3145744 | tf_op jit(solution)/shard_map/panels/all_gather | solution.py:58
  136.7 3.2 %copy.57 = bf16[1536,1024]{1,0:T(8,128)(2,1)S(1)} copy(bf16[1536,1024]{0,1:T(8,128)(2,1)} %bitcast.98) | data formatting | bytes 6291456 | tf_op jit(solution)/shard_map/gram/dot_general | solution.py:70
  139.9 2.9 %fusion.5 = f32[3,2,256,384]{3,2,1,0:T(8,128)S(1)} fusion(bf16[3,2,256,1024]{3,2,1,0:T(8,128)(2,1)S(1)} %bitcast.99, bf16[1024,384,1,1]{1,0,3,2:T(8,128)(2,1)} %bitcast.113), kind=kOutput, calls=%fused_computation.31 | convolution fusion | flops 1207959552 | bytes 6291456 | tf_op jit(solution)/shard_map/gram/dot_general | solution.py:70
  142.9 0.1 dynamic-slice_bitcast_fusion
  143.0 1.3 copy-done.1
  144.3 10.6 %collective-permute-start.1 = (f32[3,256,384]{2,1,0:T(8,128)S(1)}, f32[3,256,384]{2,1,0:T(8,128)S(1)}, u32[]{:S(2)}, u32[]{:S(2)}) collective-permute-start(f32[3,256,384]{2,1,0:T(8,128)S(1)} %dynamic-slice_bitcast_fusion), channel_id=1, source_target_pairs={{0,4},{4,0},{1,5},{5,1},{2,6},{6,2},{3,7},{7,3},{8,12},{12,8},{9,1... | collective-permute-start | bytes 3538952 | tf_op jit(solution)/shard_map/gram/ppermute | solution.py:12
  154.9 0.8 dynamic_slice.16
  155.7 0.8 dynamic_slice.15
  156.5 0.2 select_reduce_fusion
  156.7 0.7 collective-permute-done.1
  157.4 1.4 fusion.1
  158.7 0.9 copy.62
  159.6 3.5 %all-to-all-start.4 = ((bf16[4,192,384]{2,1,0:T(8,128)(2,1)}), bf16[4,192,384]{2,1,0:T(8,128)(2,1)S(1)}, u32[]{:S(2)}, u32[]{:S(2)}) async-start(bf16[4,192,384]{2,1,0:T(8,128)(2,1)} %bitcast.39), calls=%async_computation.4 | async-start | bytes 1179648 | tf_op jit(solution)/shard_map/gram/all_to_all | solution.py:18
  163.1 0.1 broadcast_add_fusion
  163.2 0.1 broadcast_subtract_fusion
  163.3 9.5 %all-to-all-done.4 = bf16[4,192,384]{2,1,0:T(8,128)(2,1)S(1)} async-done(((bf16[4,192,384]{2,1,0:T(8,128)(2,1)}), bf16[4,192,384]{2,1,0:T(8,128)(2,1)S(1)}, u32[]{:S(2)}, u32[]{:S(2)}) %all-to-all-start.4) | async-done | bytes 589856 | tf_op jit(solution)/shard_map/gram/all_to_all | solution.py:18
  172.8 0.1 convert_reduce_fusion
  172.9 0.1 reshape.179
  173.0 0.3 subtract_divide_fusion
  173.3 0.3 fusion.2
  173.5 0.1 fusion.3
  173.7 11.0 %all_gather.15 = bf16[4,192,384]{2,1,0:T(8,128)(2,1)S(1)} all-gather(bf16[1,192,384]{2,1,0:T(8,128)(2,1)S(1)} %pad_maximum_fusion.4), channel_id=1, replica_groups=mesh['x'=4,'z'=16,'c'=2,'y'=4] {'y'}, dimensions={0}, use_global_device_ids=true | all-gather | bytes 737280 | tf_op jit(solution)/shard_map/amplitudes/all_gather | solution.py:98
  184.7 0.1 copy.67
  184.8 6.0 %collective-permute-start.3 = (bf16[3,256,384]{2,1,0:T(8,128)(2,1)S(1)}, bf16[3,256,384]{2,1,0:T(8,128)(2,1)S(1)}, u32[]{:S(2)}, u32[]{:S(2)}) collective-permute-start(bf16[3,256,384]{2,1,0:T(8,128)(2,1)S(1)} %bitcast.103), channel_id=1, source_target_pairs={{0,4},{4,0},{1,5},{5,1},{2,6},{6,2},{3,7},{7,3},{8,12},{12,8},{9,1... | collective-permute-start | bytes 1769480 | tf_op jit(solution)/shard_map/amplitudes/ppermute | solution.py:12
  190.8 1.6 collective-permute-done.3
  192.4 0.2 select_bitcast_fusion.1
  192.6 0.1 pad_maximum_fusion
  192.7 0.1 copy.68
  192.8 1.6 copy-done
  194.4 1.8 convolution_convert_fusion
  196.2 0.1 copy.69
  196.3 16.3 %all_to_all.59 = bf16[4,256,384]{2,1,0:T(8,128)(2,1)S(1)} all-to-all(bf16[4,256,384]{2,1,0:T(8,128)(2,1)S(1)} %bitcast.101), channel_id=1, replica_groups=mesh['x'=4,'z'=16,'c'=2,'y'=4] {'x'}, dimensions={0} | all-to-all | bytes 1572864 | tf_op jit(solution)/shard_map/gamma/all_to_all | solution.py:18
  212.6 0.8 reduce_sum.45
  213.4 6.5 %all-to-all-start.6 = ((bf16[16,16,384]{2,1,0:T(8,128)(2,1)}), bf16[16,16,384]{2,1,0:T(8,128)(2,1)S(1)}, u32[]{:S(2)}, u32[]{:S(2)}) async-start(bf16[16,16,384]{2,1,0:T(8,128)(2,1)} %bitcast.54), calls=%async_computation.6 | async-start | bytes 393216 | tf_op jit(solution)/shard_map/gamma/all_to_all | solution.py:18
  219.9 14.2 %collective-permute-start.2 = (f32[3,64,3,128]{3,2,1,0:T(4,128)S(1)}, f32[3,64,3,128]{3,2,1,0:T(4,128)S(1)}, u32[]{:S(2)}, u32[]{:S(2)}) collective-permute-start(f32[3,64,3,128]{3,2,1,0:T(4,128)S(1)} %subtract_divide_fusion), channel_id=1, source_target_pairs={{0,0},{4,64},{8,8},{12,72},{16,16},{20,80},{24,24},{28,88},{32,32}... | collective-permute-start | bytes 884744 | tf_op jit(solution)/shard_map/amplitudes/ppermute | solution.py:96
  234.2 21.2 %collective-permute-done.2 = f32[3,64,3,128]{3,2,1,0:T(4,128)S(1)} collective-permute-done((f32[3,64,3,128]{3,2,1,0:T(4,128)S(1)}, f32[3,64,3,128]{3,2,1,0:T(4,128)S(1)}, u32[]{:S(2)}, u32[]{:S(2)}) %collective-permute-start.2) | collective-permute-done | bytes 294944 | tf_op jit(solution)/shard_map/amplitudes/ppermute | solution.py:96
  255.4 0.7 copy.71
  256.1 0.1 reshape.184
  256.2 0.2 copy.70
  256.5 0.8 reshape.185
  (22 shorter events, 0.2 us)
Async XLA Ops:
  7.2 18.2 %copy-start.2 = (bf16[64,3,640]{2,0,1:T(8,128)(2,1)S(1)}, bf16[64,3,640]{2,0,1:T(8,128)(2,1)}, u32[]{:S(2)}) copy-start(bf16[64,3,640]{2,0,1:T(8,128)(2,1)} %param.6) | copy-start | bytes 737284
  8.7 31.0 %all-to-all-start = ((bf16[16,16,640]{2,1,0:T(8,128)(2,1)}), bf16[16,16,640]{2,1,0:T(8,128)(2,1)S(1)}, u32[]{:S(2)}, u32[]{:S(2)}) async-start(bf16[16,16,640]{2,1,0:T(8,128)(2,1)} %broadcast_in_dim.10), calls=%async_computation | async-start | bytes 655360 | tf_op jit(solution)/shard_map/transform/all_to_all | solution.py:18
  24.4 112.3 %all-gather.2.cloned.1.call-start = ((), (), s32[]{:S(2)}) async-start(), calls=%async_computation.7 | async-start | bytes 3342336 | tf_op jit(solution)/shard_map/panels/all_gather | solution.py:58
  39.7 9.6 %collective-permute-start = (bf16[16,16,640]{2,1,0:T(8,128)(2,1)S(1)}, bf16[16,16,640]{2,1,0:T(8,128)(2,1)S(1)}, u32[]{:S(2)}, u32[]{:S(2)}) collective-permute-start(bf16[16,16,640]{2,1,0:T(8,128)(2,1)S(1)} %all-to-all-done), channel_id=1, source_target_pairs={{0,4},{4,0},{1,5},{5,1},{2,6},{6,2},{3,7},{7,3},{8,12},{12,8},{9,1... | collective-permute-start | bytes 983048 | tf_op jit(solution)/shard_map/transform/ppermute | solution.py:12
  76.6 21.6 %all-to-all-start.3 = ((bf16[16,16,384]{2,1,0:T(8,128)(2,1)}), bf16[16,16,384]{2,1,0:T(8,128)(2,1)S(1)}, u32[]{:S(2)}, u32[]{:S(2)}) async-start(bf16[16,16,384]{2,1,0:T(8,128)(2,1)} %pad_maximum_fusion.3), calls=%async_computation.3 | async-start | bytes 393216 | tf_op jit(solution)/shard_map/panels/all_to_all | solution.py:18
  142.9 1.5 copy-start.1
  142.9 13.6 %copy-start.3 = (f32[512]{0:T(512)S(1)}, f32[512]{0:T(512)}, u32[]{:S(2)}) copy-start(f32[512]{0:T(512)} %param.9) | copy-start | bytes 6148
  142.9 13.6 %copy-start.4 = (s32[3]{0:T(128)S(1)}, s32[3]{0:T(128)}, u32[]{:S(2)}) copy-start(s32[3]{0:T(128)} %param.11) | copy-start | bytes 40
  144.3 13.0 %collective-permute-start.1 = (f32[3,256,384]{2,1,0:T(8,128)S(1)}, f32[3,256,384]{2,1,0:T(8,128)S(1)}, u32[]{:S(2)}, u32[]{:S(2)}) collective-permute-start(f32[3,256,384]{2,1,0:T(8,128)S(1)} %dynamic-slice_bitcast_fusion), channel_id=1, source_target_pairs={{0,4},{4,0},{1,5},{5,1},{2,6},{6,2},{3,7},{7,3},{8,12},{12,8},{9,1... | collective-permute-start | bytes 3538952 | tf_op jit(solution)/shard_map/gram/ppermute | solution.py:12
  159.6 13.2 %all-to-all-start.4 = ((bf16[4,192,384]{2,1,0:T(8,128)(2,1)}), bf16[4,192,384]{2,1,0:T(8,128)(2,1)S(1)}, u32[]{:S(2)}, u32[]{:S(2)}) async-start(bf16[4,192,384]{2,1,0:T(8,128)(2,1)} %bitcast.39), calls=%async_computation.4 | async-start | bytes 1179648 | tf_op jit(solution)/shard_map/gram/all_to_all | solution.py:18
  184.8 7.6 %collective-permute-start.3 = (bf16[3,256,384]{2,1,0:T(8,128)(2,1)S(1)}, bf16[3,256,384]{2,1,0:T(8,128)(2,1)S(1)}, u32[]{:S(2)}, u32[]{:S(2)}) collective-permute-start(bf16[3,256,384]{2,1,0:T(8,128)(2,1)S(1)} %bitcast.103), channel_id=1, source_target_pairs={{0,4},{4,0},{1,5},{5,1},{2,6},{6,2},{3,7},{7,3},{8,12},{12,8},{9,1... | collective-permute-start | bytes 1769480 | tf_op jit(solution)/shard_map/amplitudes/ppermute | solution.py:12
  192.5 1.9 copy-start
  213.4 42.7 %all-to-all-start.6 = ((bf16[16,16,384]{2,1,0:T(8,128)(2,1)}), bf16[16,16,384]{2,1,0:T(8,128)(2,1)S(1)}, u32[]{:S(2)}, u32[]{:S(2)}) async-start(bf16[16,16,384]{2,1,0:T(8,128)(2,1)} %bitcast.54), calls=%async_computation.6 | async-start | bytes 393216 | tf_op jit(solution)/shard_map/gamma/all_to_all | solution.py:18
  219.9 35.5 %collective-permute-start.2 = (f32[3,64,3,128]{3,2,1,0:T(4,128)S(1)}, f32[3,64,3,128]{3,2,1,0:T(4,128)S(1)}, u32[]{:S(2)}, u32[]{:S(2)}) collective-permute-start(f32[3,64,3,128]{3,2,1,0:T(4,128)S(1)} %subtract_divide_fusion), channel_id=1, source_target_pairs={{0,0},{4,64},{8,8},{12,72},{16,16},{20,80},{24,24},{28,88},{32,32}... | collective-permute-start | bytes 884744 | tf_op jit(solution)/shard_map/amplitudes/ppermute | solution.py:96
Sparse Core Ops, SparseCore 0:
  66.7 69.9 all-gather.1
where the time goes:
time: 265 us; the launch traced here: 264 us
  blocking collectives  76.8 us (29%)
  waiting for transfers between devices  75.8 us (29%)
  starting transfers between devices  71.6 us (27%)
  between operations  14.4 us (5%)
  local copies, waits for them, and re-layouts  14 us (5%)
  other arithmetic  5.86 us (2%)
  matrix products  5.51 us (2%)
    all_to_all x3, blocking collectives, exchange(): value = lax.all_to_all(value, axis, split_axis=0, concat_axis=0, tiled=True)  40.7 us
    all_to_all x4, starting transfers between devices, exchange(): value = lax.all_to_all(value, axis, split_axis=0, concat_axis=0, tiled=True)  32.4 us
    all_gather x1, waiting for transfers between devices, local(): lax.all_gather(row.reshape(nx * r, nocc * wide), 'z', axis=0, tiled=True)  25.6 us
    all_to_all x4, waiting for transfers between devices, exchange(): value = lax.all_to_all(value, axis, split_axis=0, concat_axis=0, tiled=True)  25.5 us
    ppermute x3, starting transfers between devices, swap_cores(): return lax.ppermute(value, 'c', [(0, 1), (1, 0)])  25 us
    ppermute x1, waiting for transfers between devices, local(): own = lax.ppermute(amps, ('z', 'c'), swap)  21.2 us
    ppermute x1, starting transfers between devices, local(): own = lax.ppermute(amps, ('z', 'c'), swap)  14.2 us
    all_gather x1, blocking collectives, local(): masked = lax.all_gather(masked.reshape(-1, ao_part), 'x', axis=0)  13.2 us
  transfers between devices with their start and end apart: 9, of which 8 were waited for; matrix products, arithmetic and copies ran while one was open for 2% of the time, Pallas kernels for 0%

commit v1 on v0

--- a/solution.py
+++ b/solution.py
@@ -55,7 +55,12 @@
         three = jnp.sum(part.astype(F32), axis=0).astype(BF).reshape(nx, nocc, r, wide)
     with jax.named_scope("panels"):
         row = jnp.concatenate([three[:, i] for i in range(nocc)], axis=-1)
-        row = lax.all_gather(row.reshape(nx * r, nocc * wide), "z", axis=0, tiled=True)
+        row = jnp.concatenate(
+            lax.all_to_all(
+                jnp.stack([row.reshape(nx * r, nocc * wide)] * lax.axis_size("z")), "z", 0, 0
+            ),
+            axis=0,
+        )
         col = exchange(three.reshape(nx, nocc * r, wide), "x")
         col = col.reshape(nx, nocc, r, ways // 2, 2, narrow)
         col = jnp.concatenate(

time: 265 us -> 356 us (1.34)
  waiting for transfers between devices: 75.8 us -> 173 us
  between operations: 14.4 us -> 1 us
  starting transfers between devices: 71.6 us -> 75.4 us
    all_to_all x0 -> x1, waiting for transfers between devices: none -> 125 us  [local(): lax.all_to_all(jnp.stack([row.reshape(nx * r, nocc * wide)] * lax.axis_si...]
    all_gather x1 -> x0, waiting for transfers between devices: 25.6 us -> none  [local(): lax.all_gather(row.reshape(nx * r, nocc * wide), 'z', axis=0, tiled=True)]
    ppermute x3, starting transfers between devices: 25 us -> 18.1 us  [swap_cores(): return lax.ppermute(value, 'c', [(0, 1), (1, 0)])]
    all_to_all x0 -> x1, starting transfers between devices: none -> 6.08 us  [local(): lax.all_to_all(jnp.stack([row.reshape(nx * r, nocc * wide)] * lax.axis_si...]
    all_to_all x4, starting transfers between devices: 32.4 us -> 37.6 us  [exchange(): value = lax.all_to_all(value, axis, split_axis=0, concat_axis=0, tiled=True)]
    all_to_all x4, waiting for transfers between devices: 25.5 us -> 21.6 us  [exchange(): value = lax.all_to_all(value, axis, split_axis=0, concat_axis=0, tiled=True)]
where the time goes in v1:
time: 356 us; the launch traced here: 355 us
  waiting for transfers between devices  173 us (49%)
  starting transfers between devices  75.4 us (21%)
  blocking collectives  73.5 us (21%)
  local copies, waits for them, and re-layouts  15.8 us (4%)
  other arithmetic  9.24 us (3%)
  matrix products  6.47 us (2%)
    all_to_all x1, waiting for transfers between devices, local(): lax.all_to_all(jnp.stack([row.reshape(nx * r, nocc * wide)] * lax.axis_si...  125 us
    all_to_all x3, blocking collectives, exchange(): value = lax.all_to_all(value, axis, split_axis=0, concat_axis=0, tiled=True)  38.9 us
    all_to_all x4, starting transfers between devices, exchange(): value = lax.all_to_all(value, axis, split_axis=0, concat_axis=0, tiled=True)  37.6 us
    ppermute x1, waiting for transfers between devices, local(): own = lax.ppermute(amps, ('z', 'c'), swap)  22.9 us
    all_to_all x4, waiting for transfers between devices, exchange(): value = lax.all_to_all(value, axis, split_axis=0, concat_axis=0, tiled=True)  21.6 us
    ppermute x3, starting transfers between devices, swap_cores(): return lax.ppermute(value, 'c', [(0, 1), (1, 0)])  18.1 us
    ppermute x1, starting transfers between devices, local(): own = lax.ppermute(amps, ('z', 'c'), swap)  13.6 us
    all_gather x1, blocking collectives, local(): masked = lax.all_gather(masked.reshape(-1, ao_part), 'x', axis=0)  13.2 us
  transfers between devices with their start and end apart: 9, of which 8 were waited for; matrix products, arithmetic and copies ran while one was open for 2% of the time, Pallas kernels for 0%

profile of v1, /device:TPU:1, one launch (start us, length us, event | category | flops | bytes accessed | tf_op | source)
XLA Modules:
  0.0 354.6 jit_solution(8689925527877326871)
XLA Ops:
  0.6 1.5 broadcast_in_dim.10
  2.1 15.7 %all-to-all-start = ((bf16[16,16,640]{2,1,0:T(8,128)(2,1)}), bf16[16,16,640]{2,1,0:T(8,128)(2,1)S(1)}, u32[]{:S(2)}, u32[]{:S(2)}) async-start(bf16[16,16,640]{2,1,0:T(8,128)(2,1)} %broadcast_in_dim.10), calls=%async_computation | async-start | bytes 655360 | tf_op jit(solution)/shard_map/transform/all_to_all | solution.py:18
  17.9 0.7 convert_element_type.44
  18.6 0.1 broadcast_in_dim.9
  18.7 1.0 broadcast_multiply_fusion
  19.7 13.2 %all_gather.9 = bf16[4,192,640]{2,1,0:T(8,128)(2,1)S(1)} all-gather(bf16[1,192,640]{2,1,0:T(8,128)(2,1)S(1)} %bitcast.116), channel_id=1, replica_groups=mesh['x'=4,'z'=16,'c'=2,'y'=4] {'x'}, dimensions={0}, use_global_device_ids=true | all-gather | bytes 1228800 | tf_op jit(solution)/shard_map/transform/all_gather | solution.py:48
  33.0 0.1 all-to-all-done
  33.1 8.4 %collective-permute-start = (bf16[16,16,640]{2,1,0:T(8,128)(2,1)S(1)}, bf16[16,16,640]{2,1,0:T(8,128)(2,1)S(1)}, u32[]{:S(2)}, u32[]{:S(2)}) collective-permute-start(bf16[16,16,640]{2,1,0:T(8,128)(2,1)S(1)} %all-to-all-done), channel_id=1, source_target_pairs={{0,4},{4,0},{1,5},{5,1},{2,6},{6,2},{3,7},{7,3},{8,12},{12,8},{9,1... | collective-permute-start | bytes 983048 | tf_op jit(solution)/shard_map/transform/ppermute | solution.py:12
  41.5 1.2 collective-permute-done
  42.7 0.1 select_bitcast_fusion.3
  42.8 0.1 pad_maximum_fusion.1
  42.9 0.8 fusion
  43.7 0.1 copy.56
  43.8 15.4 %all_to_all.62 = bf16[4,192,512]{2,1,0:T(8,128)(2,1)S(1)} all-to-all(bf16[4,192,512]{2,1,0:T(8,128)(2,1)S(1)} %bitcast.105), channel_id=1, replica_groups=mesh['x'=4,'z'=16,'c'=2,'y'=4] {'y'}, dimensions={0} | all-to-all | bytes 1572864 | tf_op jit(solution)/shard_map/transform/all_to_all | solution.py:18
  59.2 0.1 reduce_sum.42
  59.3 9.0 %all_to_all.63 = bf16[4,48,512]{2,1,0:T(8,128)(2,1)S(1)} all-to-all(bf16[4,48,512]{2,1,0:T(8,128)(2,1)S(1)} %bitcast.112), channel_id=1, replica_groups=mesh['x'=4,'z'=16,'c'=2,'y'=4] {'x'}, dimensions={0} | all-to-all | bytes 393216 | tf_op jit(solution)/shard_map/panels/all_to_all | solution.py:18
  68.3 0.1 reshape.198
  68.4 0.2 slice_bitcast_fusion.2
  68.6 0.7 pad_maximum_fusion.2
  69.3 7.6 %all-to-all-start.4 = ((bf16[16,16,384]{2,1,0:T(8,128)(2,1)}), bf16[16,16,384]{2,1,0:T(8,128)(2,1)S(1)}, u32[]{:S(2)}, u32[]{:S(2)}) async-start(bf16[16,16,384]{2,1,0:T(8,128)(2,1)} %pad_maximum_fusion.2), calls=%async_computation.4 | async-start | bytes 393216 | tf_op jit(solution)/shard_map/panels/all_to_all | solution.py:18
  76.9 12.3 %all-to-all-done.4 = bf16[16,16,384]{2,1,0:T(8,128)(2,1)S(1)} async-done(((bf16[16,16,384]{2,1,0:T(8,128)(2,1)}), bf16[16,16,384]{2,1,0:T(8,128)(2,1)S(1)}, u32[]{:S(2)}, u32[]{:S(2)}) %all-to-all-start.4) | async-done | bytes 196640 | tf_op jit(solution)/shard_map/panels/all_to_all | solution.py:18
  89.2 1.9 stack.24
  91.1 6.1 %all-to-all-start.2 = ((bf16[16,64,1536]{2,1,0:T(8,128)(2,1)}), bf16[16,64,1536]{2,1,0:T(8,128)(2,1)S(1)}, u32[]{:S(2)}, u32[]{:S(2)}) async-start(bf16[16,64,1536]{2,1,0:T(8,128)(2,1)} %stack.24), calls=%async_computation.2 | async-start | bytes 6291456 | tf_op jit(solution)/shard_map/panels/all_to_all | solution.py:59
  97.2 11.0 %all_gather.10 = bf16[4,256,384]{2,1,0:T(8,128)(2,1)S(1)} all-gather(bf16[1,256,384]{2,1,0:T(8,128)(2,1)S(1)} %bitcast.121), channel_id=1, replica_groups=mesh['x'=4,'z'=16,'c'=2,'y'=4] {'x'}, dimensions={0}, use_global_device_ids=true | all-gather | bytes 983040 | tf_op jit(solution)/shard_map/panels/all_gather | solution.py:71
  108.2 1.0 copy.61
  109.2 124.8 %all-to-all-done.2 = bf16[16,64,1536]{2,1,0:T(8,128)(2,1)S(1)} async-done(((bf16[16,64,1536]{2,1,0:T(8,128)(2,1)}), bf16[16,64,1536]{2,1,0:T(8,128)(2,1)S(1)}, u32[]{:S(2)}, u32[]{:S(2)}) %all-to-all-start.2) | async-done | bytes 3145760 | tf_op jit(solution)/shard_map/panels/all_to_all | solution.py:59
  234.0 2.9 copy.57
  236.9 3.9 %fusion.5 = f32[3,2,256,384]{3,2,1,0:T(8,128)S(1)} fusion(bf16[3,2,256,1024]{3,2,1,0:T(8,128)(2,1)} %bitcast.104, bf16[1024,384,1,1]{1,0,3,2:T(8,128)(2,1)} %bitcast.119), kind=kOutput, calls=%fused_computation.31 | convolution fusion | flops 1207959552 | bytes 6291456 | tf_op jit(solution)/shard_map/gram/dot_general | solution.py:75
  240.8 1.4 copy-done
  242.2 1.1 dynamic-slice_bitcast_fusion
  243.3 3.4 collective-permute-start.1
  246.7 0.8 dynamic_slice.16
  247.5 0.8 dynamic_slice.15
  248.3 0.2 select_reduce_fusion
  248.4 1.0 collective-permute-done.1
  249.5 1.7 fusion.1
  251.2 0.9 copy.62
  252.1 4.1 %all-to-all-start.5 = ((bf16[4,192,384]{2,1,0:T(8,128)(2,1)}), bf16[4,192,384]{2,1,0:T(8,128)(2,1)}, u32[]{:S(2)}, u32[]{:S(2)}) async-start(bf16[4,192,384]{2,1,0:T(8,128)(2,1)} %bitcast.109), calls=%async_computation.5 | async-start | bytes 1179648 | tf_op jit(solution)/shard_map/gram/all_to_all | solution.py:18
  256.3 0.1 broadcast_add_fusion
  256.3 0.7 broadcast_subtract_fusion
  257.1 9.2 %all-to-all-done.5 = bf16[4,192,384]{2,1,0:T(8,128)(2,1)} async-done(((bf16[4,192,384]{2,1,0:T(8,128)(2,1)}), bf16[4,192,384]{2,1,0:T(8,128)(2,1)}, u32[]{:S(2)}, u32[]{:S(2)}) %all-to-all-start.5) | async-done | bytes 589856 | tf_op jit(solution)/shard_map/gram/all_to_all | solution.py:18
  266.3 1.2 convert_reduce_fusion
  267.4 0.9 reshape.202
  268.3 1.3 subtract_divide_fusion
  269.6 0.3 fusion.2
  269.9 0.1 fusion.3
  270.0 10.4 %all_gather.11 = bf16[4,192,384]{2,1,0:T(8,128)(2,1)S(1)} all-gather(bf16[1,192,384]{2,1,0:T(8,128)(2,1)S(1)} %pad_maximum_fusion.3), channel_id=1, replica_groups=mesh['x'=4,'z'=16,'c'=2,'y'=4] {'y'}, dimensions={0}, use_global_device_ids=true | all-gather | bytes 737280 | tf_op jit(solution)/shard_map/amplitudes/all_gather | solution.py:103
  280.4 0.1 copy.67
  280.5 6.3 %collective-permute-start.3 = (bf16[3,256,384]{2,1,0:T(8,128)(2,1)S(1)}, bf16[3,256,384]{2,1,0:T(8,128)(2,1)S(1)}, u32[]{:S(2)}, u32[]{:S(2)}) collective-permute-start(bf16[3,256,384]{2,1,0:T(8,128)(2,1)S(1)} %bitcast.108), channel_id=1, source_target_pairs={{0,4},{4,0},{1,5},{5,1},{2,6},{6,2},{3,7},{7,3},{8,12},{12,8},{9,1... | collective-permute-start | bytes 1769480 | tf_op jit(solution)/shard_map/amplitudes/ppermute | solution.py:12
  286.8 1.6 collective-permute-done.3
  288.4 0.2 select_bitcast_fusion.1
  288.6 0.1 pad_maximum_fusion
  288.7 0.1 copy.68
  288.9 1.8 convolution_convert_fusion
  290.7 0.1 copy.69
  290.7 14.4 %all_to_all.64 = bf16[4,256,384]{2,1,0:T(8,128)(2,1)S(1)} all-to-all(bf16[4,256,384]{2,1,0:T(8,128)(2,1)S(1)} %bitcast.106), channel_id=1, replica_groups=mesh['x'=4,'z'=16,'c'=2,'y'=4] {'x'}, dimensions={0} | all-to-all | bytes 1572864 | tf_op jit(solution)/shard_map/gamma/all_to_all | solution.py:18
  305.2 0.8 reduce_sum.45
  306.0 10.2 %all-to-all-start.7 = ((bf16[16,16,384]{2,1,0:T(8,128)(2,1)}), bf16[16,16,384]{2,1,0:T(8,128)(2,1)S(1)}, u32[]{:S(2)}, u32[]{:S(2)}) async-start(bf16[16,16,384]{2,1,0:T(8,128)(2,1)} %bitcast.56), calls=%async_computation.7 | async-start | bytes 393216 | tf_op jit(solution)/shard_map/gamma/all_to_all | solution.py:18
  316.2 13.6 %collective-permute-start.2 = (f32[3,64,3,128]{3,2,1,0:T(4,128)S(1)}, f32[3,64,3,128]{3,2,1,0:T(4,128)S(1)}, u32[]{:S(2)}, u32[]{:S(2)}) collective-permute-start(f32[3,64,3,128]{3,2,1,0:T(4,128)S(1)} %subtract_divide_fusion), channel_id=1, source_target_pairs={{0,0},{4,64},{8,8},{12,72},{16,16},{20,80},{24,24},{28,88},{32,32}... | collective-permute-start | bytes 884744 | tf_op jit(solution)/shard_map/amplitudes/ppermute | solution.py:101
  329.8 22.9 %collective-permute-done.2 = f32[3,64,3,128]{3,2,1,0:T(4,128)S(1)} collective-permute-done((f32[3,64,3,128]{3,2,1,0:T(4,128)S(1)}, f32[3,64,3,128]{3,2,1,0:T(4,128)S(1)}, u32[]{:S(2)}, u32[]{:S(2)}) %collective-permute-start.2) | collective-permute-done | bytes 294944 | tf_op jit(solution)/shard_map/amplitudes/ppermute | solution.py:101
  352.7 0.7 copy.71
  353.5 0.1 reshape.207
  353.5 0.2 copy.70
  353.8 0.8 reshape.208
  (18 shorter events, 0.2 us)
Async XLA Ops:
  2.1 31.0 %all-to-all-start = ((bf16[16,16,640]{2,1,0:T(8,128)(2,1)}), bf16[16,16,640]{2,1,0:T(8,128)(2,1)S(1)}, u32[]{:S(2)}, u32[]{:S(2)}) async-start(bf16[16,16,640]{2,1,0:T(8,128)(2,1)} %broadcast_in_dim.10), calls=%async_computation | async-start | bytes 655360 | tf_op jit(solution)/shard_map/transform/all_to_all | solution.py:18
  33.1 9.6 %collective-permute-start = (bf16[16,16,640]{2,1,0:T(8,128)(2,1)S(1)}, bf16[16,16,640]{2,1,0:T(8,128)(2,1)S(1)}, u32[]{:S(2)}, u32[]{:S(2)}) collective-permute-start(bf16[16,16,640]{2,1,0:T(8,128)(2,1)S(1)} %all-to-all-done), channel_id=1, source_target_pairs={{0,4},{4,0},{1,5},{5,1},{2,6},{6,2},{3,7},{7,3},{8,12},{12,8},{9,1... | collective-permute-start | bytes 983048 | tf_op jit(solution)/shard_map/transform/ppermute | solution.py:12
  69.3 19.9 %all-to-all-start.4 = ((bf16[16,16,384]{2,1,0:T(8,128)(2,1)}), bf16[16,16,384]{2,1,0:T(8,128)(2,1)S(1)}, u32[]{:S(2)}, u32[]{:S(2)}) async-start(bf16[16,16,384]{2,1,0:T(8,128)(2,1)} %pad_maximum_fusion.2), calls=%async_computation.4 | async-start | bytes 393216 | tf_op jit(solution)/shard_map/panels/all_to_all | solution.py:18
  91.1 142.9 %all-to-all-start.2 = ((bf16[16,64,1536]{2,1,0:T(8,128)(2,1)}), bf16[16,64,1536]{2,1,0:T(8,128)(2,1)S(1)}, u32[]{:S(2)}, u32[]{:S(2)}) async-start(bf16[16,64,1536]{2,1,0:T(8,128)(2,1)} %stack.24), calls=%async_computation.2 | async-start | bytes 6291456 | tf_op jit(solution)/shard_map/panels/all_to_all | solution.py:59
  240.8 1.4 copy-start
  242.2 6.0 %copy-start.1 = (f32[512]{0:T(512)S(1)}, f32[512]{0:T(512)}, u32[]{:S(2)}) copy-start(f32[512]{0:T(512)} %param.9) | copy-start | bytes 6148
  242.2 6.0 %copy-start.2 = (s32[3]{0:T(128)S(1)}, s32[3]{0:T(128)}, u32[]{:S(2)}) copy-start(s32[3]{0:T(128)} %param.11) | copy-start | bytes 40
  243.3 6.2 %collective-permute-start.1 = (f32[3,256,384]{2,1,0:T(8,128)}, f32[3,256,384]{2,1,0:T(8,128)}, u32[]{:S(2)}, u32[]{:S(2)}) collective-permute-start(f32[3,256,384]{2,1,0:T(8,128)} %dynamic-slice_bitcast_fusion), channel_id=1, source_target_pairs={{0,4},{4,0},{1,5},{5,1},{2,6},{6,2},{3,7},{7,3},{8,12},{12,8},{9,1... | collective-permute-start | bytes 3538952 | tf_op jit(solution)/shard_map/gram/ppermute | solution.py:12
  252.1 14.1 %all-to-all-start.5 = ((bf16[4,192,384]{2,1,0:T(8,128)(2,1)}), bf16[4,192,384]{2,1,0:T(8,128)(2,1)}, u32[]{:S(2)}, u32[]{:S(2)}) async-start(bf16[4,192,384]{2,1,0:T(8,128)(2,1)} %bitcast.109), calls=%async_computation.5 | async-start | bytes 1179648 | tf_op jit(solution)/shard_map/gram/all_to_all | solution.py:18
  280.5 7.9 %collective-permute-start.3 = (bf16[3,256,384]{2,1,0:T(8,128)(2,1)S(1)}, bf16[3,256,384]{2,1,0:T(8,128)(2,1)S(1)}, u32[]{:S(2)}, u32[]{:S(2)}) collective-permute-start(bf16[3,256,384]{2,1,0:T(8,128)(2,1)S(1)} %bitcast.108), channel_id=1, source_target_pairs={{0,4},{4,0},{1,5},{5,1},{2,6},{6,2},{3,7},{7,3},{8,12},{12,8},{9,1... | collective-permute-start | bytes 1769480 | tf_op jit(solution)/shard_map/amplitudes/ppermute | solution.py:12
  306.0 47.4 %all-to-all-start.7 = ((bf16[16,16,384]{2,1,0:T(8,128)(2,1)}), bf16[16,16,384]{2,1,0:T(8,128)(2,1)S(1)}, u32[]{:S(2)}, u32[]{:S(2)}) async-start(bf16[16,16,384]{2,1,0:T(8,128)(2,1)} %bitcast.56), calls=%async_computation.7 | async-start | bytes 393216 | tf_op jit(solution)/shard_map/gamma/all_to_all | solution.py:18
  316.2 36.5 %collective-permute-start.2 = (f32[3,64,3,128]{3,2,1,0:T(4,128)S(1)}, f32[3,64,3,128]{3,2,1,0:T(4,128)S(1)}, u32[]{:S(2)}, u32[]{:S(2)}) collective-permute-start(f32[3,64,3,128]{3,2,1,0:T(4,128)S(1)} %subtract_divide_fusion), channel_id=1, source_target_pairs={{0,0},{4,64},{8,8},{12,72},{16,16},{20,80},{24,24},{28,88},{32,32}... | collective-permute-start | bytes 884744 | tf_op jit(solution)/shard_map/amplitudes/ppermute | solution.py:101
